TPU v7x, 32 devices: a whole 2x2x4 slice. The times are simulated.
32 devices in a mesh: dp: 8 (over z, x), tensor: 4 (over y, core).
Axes of the slice: x: 2, y: 2, z: 4, core: 2. Of those that a mesh axis runs over, the one named last changes fastest.
Arguments:
- hidden_in: bfloat16 [32768, 768], P(('dp', 'tensor')), may hold values from -6 to 6
- teacher: float32 [32768, 768], P(('dp', 'tensor')), may hold values from -6 to 6
- valid_mask: int32 [32768], P(('dp', 'tensor')), may hold values from 0 to 1
- random_blocks: int32 [12, 32, 3, 32], replicated, may hold values from 0 to 1, as said below
- w_qkv: bfloat16 [3, 768, 768], P(None, 'dp', 'tensor'), may hold values from -0.21875 to 0.21875
- b_qv: bfloat16 [2, 12, 64], P(None, 'tensor', 'dp'), may hold values from -3 to 3
- w_out: bfloat16 [768, 768], P('tensor', 'dp'), may hold values from -3 to 3
- w_in: bfloat16 [768, 3072], P('dp', 'tensor'), may hold values from -0.21875 to 0.21875
- b_in: bfloat16 [48, 64], P('tensor', 'dp'), may hold values from -3 to 3
- w_back: bfloat16 [3072, 768], P('tensor', 'dp'), may hold values from -0.109375 to 0.109375
- ln_gains: bfloat16 [2, 768], P(None, 'dp'), may hold values from 0.25 to 1.75
- row_biases: bfloat16 [4, 768], P(None, 'dp'), may hold values from -2 to 2
Outputs:
- loss: float32 [], replicated
- encoded: float32 [32768, 768], P(('dp', 'tensor'))
- grad_in: float32 [32768, 768], P(('dp', 'tensor'))
- grad_qkv: float32 [3, 768, 768], P(None, 'dp', 'tensor')
- grad_qv_bias: float32 [2, 12, 64], P(None, 'tensor', 'dp')
- grad_out: float32 [768, 768], P('tensor', 'dp')
- grad_w_in: float32 [768, 3072], P('dp', 'tensor')
- grad_b_in: float32 [48, 64], P('tensor', 'dp')
- grad_w_back: float32 [3072, 768], P('tensor', 'dp')
- grad_gains: float32 [2, 768], P(None, ('dp', 'tensor'))
- grad_biases: float32 [4, 768], P(None, ('dp', 'tensor'))
Inputs may be any that keep to these rules, and one draw needn't show every extreme that they name: `random_blocks`: each [h, j, r, :] holds a single 1; the 3 blocks chosen for one h and j are different, and none of them is block 0, block 31, or within one block of j.
All inputs are finite; a program needn't handle non-finite values.
Results may differ from a plain program's by a relative error of at most 0.015.
Values may be sent and summed in bfloat16 or wider, within the bound.
A program may use at most 192 MiB of HBM per device.

v0:
```python
import jax
import jax.numpy as jnp
from jax import lax
from jax.sharding import PartitionSpec as P

D = 768
HD = 64
BLK = 64
SEQ_LEN = 2048
epsilon = 1e-06
masked_score = -1e30
exact_precision = lax.Precision.HIGHEST


def layer_norm(values, gain, shift):
    centred = values - jnp.mean(values, axis=-1, keepdims=True)
    variance = jnp.mean(centred * centred, axis=-1, keepdims=True)
    return centred * lax.rsqrt(variance + epsilon) * gain + shift


def gelu_tanh(values):
    return (
        0.5
        * values
        * (1.0 + jnp.tanh(0.7978845608028654 * (values + 0.044715 * values * values * values)))
    )


def fetch_weights(w_qkv, b_qv, w_out, w_in, b_in, w_back, ln_gains, row_biases):
    return (
        lax.all_gather(w_qkv, "dp", axis=1, tiled=True),
        lax.all_gather(b_qv, "dp", axis=2, tiled=True),
        lax.all_gather(w_out, "dp", axis=1, tiled=True),
        lax.all_gather(w_in, "dp", axis=0, tiled=True),
        lax.all_gather(b_in, "dp", axis=1, tiled=True),
        lax.all_gather(w_back, "dp", axis=1, tiled=True),
        lax.all_gather(ln_gains, "dp", axis=1, tiled=True),
        lax.all_gather(row_biases, "dp", axis=1, tiled=True),
    )


def widen_units(in_weight, in_bias, back_weight):
    return (
        lax.all_gather(in_weight, "tensor", axis=1, tiled=True),
        lax.all_gather(in_bias, "tensor", axis=0, tiled=True),
        lax.all_gather(back_weight, "tensor", axis=0, tiled=True),
    )


def gather_slots(blocks, one_hot):
    middle = one_hot.shape[0]
    nearby = jnp.stack([blocks[0:middle], blocks[1 : middle + 1], blocks[2 : middle + 2]], axis=1)
    edges = jnp.broadcast_to(
        jnp.stack([blocks[0], blocks[-1]])[None], (middle, 2) + blocks.shape[1:]
    )
    distant = jnp.einsum(
        "mrn,nbd->mrbd", one_hot, blocks, preferred_element_type=jnp.float32
    ).astype(jnp.bfloat16)
    slots = jnp.concatenate([nearby, edges, distant], axis=1)
    return slots.reshape(middle, -1, blocks.shape[-1])


def slot_valid(middle, width):
    slot_ids = jnp.arange(width) // BLK
    row_ids = jnp.arange(middle)[:, None]
    first_double = (slot_ids[None, :] == 3) & (row_ids == 0)
    last_double = (slot_ids[None, :] == 4) & (row_ids == middle - 1)
    return jnp.logical_not(first_double | last_double)[:, None, :]


def spread_slots(slot_grads, one_hot):
    middle = slot_grads.shape[0]
    parts_grad = slot_grads.reshape(middle, -1, BLK, slot_grads.shape[-1])
    nearby = (
        jnp.pad(parts_grad[:, 0], ((0, 2), (0, 0), (0, 0)))
        + jnp.pad(parts_grad[:, 1], ((1, 1), (0, 0), (0, 0)))
        + jnp.pad(parts_grad[:, 2], ((2, 0), (0, 0), (0, 0)))
    )
    edges = jnp.concatenate(
        [
            jnp.sum(parts_grad[:, 3], axis=0)[None],
            jnp.zeros((middle,) + parts_grad.shape[2:], jnp.float32),
            jnp.sum(parts_grad[:, 4], axis=0)[None],
        ],
        axis=0,
    )
    distant = jnp.einsum(
        "mrn,mrbd->nbd", one_hot.astype(jnp.float32), parts_grad[:, 5:], precision=exact_precision
    )
    return nearby + edges + distant


def log_total(scores):
    peak = jnp.max(scores, axis=-1, keepdims=True)
    return peak + jnp.log(jnp.sum(jnp.exp(scores - peak), axis=-1, keepdims=True))


def middle_scores(stack, chosen):
    queries, keys, values = (stack[0], stack[1], stack[2])
    scale = queries.shape[-1] ** (-0.5)
    one_hot = chosen[1:-1].astype(jnp.bfloat16)
    mid_queries = queries[1:-1]
    key_slots = gather_slots(keys, one_hot)
    value_slots = gather_slots(values, one_hot)
    scores = (
        jnp.einsum("mqd,mkd->mqk", mid_queries, key_slots, preferred_element_type=jnp.float32)
        * scale
    )
    scores = jnp.where(slot_valid(mid_queries.shape[0], key_slots.shape[1]), scores, masked_score)
    return (mid_queries, key_slots, value_slots, scores)


def edge_scores_of(stack):
    queries, keys, values = (stack[0], stack[1], stack[2])
    head_dim = queries.shape[-1]
    edge_queries = jnp.concatenate([queries[0], queries[-1]], axis=0)
    flat_keys = keys.reshape(-1, head_dim)
    flat_values = values.reshape(-1, head_dim)
    scores = jnp.einsum(
        "qd,kd->qk", edge_queries, flat_keys, preferred_element_type=jnp.float32
    ) * head_dim ** (-0.5)
    return (edge_queries, flat_keys, flat_values, scores)


def item_forward(stack, chosen):
    mid_queries, key_slots, value_slots, scores = middle_scores(stack, chosen)
    log_middle = log_total(scores)
    shares = jnp.exp(scores - log_middle).astype(jnp.bfloat16)
    context_mid = jnp.einsum(
        "mqk,mkd->mqd", shares, value_slots, preferred_element_type=jnp.float32
    )
    edge_queries, flat_keys, flat_values, edge_scores = edge_scores_of(stack)
    log_edge = log_total(edge_scores)
    edge_shares = jnp.exp(edge_scores - log_edge).astype(jnp.bfloat16)
    context_edge = jnp.dot(edge_shares, flat_values, preferred_element_type=jnp.float32)
    block = stack.shape[2]
    context = jnp.concatenate(
        [context_edge[:block][None], context_mid, context_edge[block:][None]], axis=0
    )
    return (context.astype(jnp.bfloat16), log_middle[..., 0], log_edge[:, 0])


def item_backward(stack, chosen, grad_context, log_middle, log_edge):
    scale = stack.shape[-1] ** (-0.5)
    block = stack.shape[2]
    mid_queries, key_slots, value_slots, scores = middle_scores(stack, chosen)
    shares = jnp.exp(scores - log_middle[..., None])
    grad_mid = grad_context[1:-1]
    grad_shares = jnp.einsum(
        "mqd,mkd->mqk", grad_mid, value_slots, preferred_element_type=jnp.float32
    )
    inner = jnp.sum(shares * grad_shares, axis=-1, keepdims=True)
    grad_scores = (shares * (grad_shares - inner)).astype(jnp.bfloat16)
    grad_query_mid = (
        jnp.einsum("mqk,mkd->mqd", grad_scores, key_slots, preferred_element_type=jnp.float32)
        * scale
    )
    grad_key_slots = (
        jnp.einsum("mqk,mqd->mkd", grad_scores, mid_queries, preferred_element_type=jnp.float32)
        * scale
    )
    grad_value_slots = jnp.einsum(
        "mqk,mqd->mkd", shares.astype(jnp.bfloat16), grad_mid, preferred_element_type=jnp.float32
    )
    edge_queries, flat_keys, flat_values, edge_scores = edge_scores_of(stack)
    edge_shares = jnp.exp(edge_scores - log_edge[:, None])
    grad_edge = jnp.concatenate([grad_context[0], grad_context[-1]], axis=0)
    grad_edge_shares = jnp.einsum(
        "qd,kd->qk", grad_edge, flat_values, preferred_element_type=jnp.float32
    )
    edge_inner = jnp.sum(edge_shares * grad_edge_shares, axis=-1, keepdims=True)
    grad_edge_scores = (edge_shares * (grad_edge_shares - edge_inner)).astype(jnp.bfloat16)
    grad_query_edge = (
        jnp.dot(grad_edge_scores, flat_keys, preferred_element_type=jnp.float32) * scale
    )
    grad_key_edge = (
        jnp.einsum("qk,qd->kd", grad_edge_scores, edge_queries, preferred_element_type=jnp.float32)
        * scale
    )
    grad_value_edge = jnp.einsum(
        "qk,qd->kd", edge_shares.astype(jnp.bfloat16), grad_edge, preferred_element_type=jnp.float32
    )
    one_hot = chosen[1:-1]
    grad_queries = jnp.concatenate(
        [grad_query_edge[:block][None], grad_query_mid, grad_query_edge[block:][None]], axis=0
    )
    grad_keys = spread_slots(grad_key_slots, one_hot) + grad_key_edge.reshape(stack.shape[1:])
    grad_values = spread_slots(grad_value_slots, one_hot) + grad_value_edge.reshape(stack.shape[1:])
    return jnp.stack([grad_queries, grad_keys, grad_values]).astype(jnp.bfloat16)


def run_forward(pair):
    return item_forward(pair[0], pair[1])


def run_backward(group_items):
    return item_backward(
        group_items[0], group_items[1], group_items[2], group_items[3], group_items[4]
    )


def per_device(
    hidden_in,
    teacher,
    valid_mask,
    random_blocks,
    w_qkv,
    b_qv,
    w_out,
    w_in,
    b_in,
    w_back,
    ln_gains,
    row_biases,
):
    local_rows = hidden_in.shape[0]
    tensor_count = lax.axis_size("tensor")
    tokens_total = local_rows * tensor_count * lax.axis_size("dp")
    group_rows = local_rows * tensor_count
    seq_count = group_rows // SEQ_LEN
    blocks_count = SEQ_LEN // BLK
    fetched = fetch_weights(w_qkv, b_qv, w_out, w_in, b_in, w_back, ln_gains, row_biases)
    qkv_weight, bias_pair, out_weight, in_weight, in_bias, back_weight, gains, biases = fetched
    full_in, full_bias, full_back = widen_units(in_weight, in_bias, back_weight)
    head_local = qkv_weight.shape[2] // HD
    chosen_local = lax.dynamic_slice_in_dim(
        random_blocks, lax.axis_index("tensor") * head_local, head_local, 0
    )
    whole_in = lax.all_gather(hidden_in, "tensor", axis=0, tiled=True)
    projected = jnp.einsum("nd,kde->kne", whole_in, qkv_weight, preferred_element_type=jnp.float32)
    bias_flat = bias_pair.astype(jnp.float32).reshape(2, -1)
    bias_rows = jnp.stack([bias_flat[0], jnp.zeros_like(bias_flat[0]), bias_flat[1]])
    projected = (projected + bias_rows[:, None, :]).astype(jnp.bfloat16)
    items = projected.reshape(3, seq_count, blocks_count, BLK, head_local, HD).transpose(
        1, 4, 0, 2, 3, 5
    )
    items = items.reshape(seq_count * head_local, 3, blocks_count, BLK, HD)
    chosen_all = jnp.tile(chosen_local, (seq_count, 1, 1, 1))
    context_items, log_middle, log_edge = lax.map(run_forward, (items, chosen_all))
    context = context_items.reshape(seq_count, head_local, blocks_count, BLK, HD).transpose(
        0, 2, 3, 1, 4
    )
    context = context.reshape(group_rows, head_local * HD)
    piece = context
    attention = lax.psum_scatter(
        jnp.dot(piece, out_weight, preferred_element_type=jnp.float32).astype(jnp.bfloat16),
        "tensor",
        scatter_dimension=0,
        tiled=True,
    ).astype(jnp.float32)
    gain_values = gains.astype(jnp.float32)
    bias_values = biases.astype(jnp.float32)
    mixed = hidden_in.astype(jnp.float32) + attention + bias_values[0]
    normed, first_back = jax.vjp(layer_norm, mixed, gain_values[0], bias_values[1])
    normed_low = normed.astype(jnp.bfloat16)
    inner = jnp.dot(normed_low, full_in, preferred_element_type=jnp.float32) + full_bias.astype(
        jnp.float32
    ).reshape(-1)
    active_float, gelu_back = jax.vjp(gelu_tanh, inner)
    active = active_float.astype(jnp.bfloat16)
    feed = jnp.dot(active, full_back, preferred_element_type=jnp.float32)
    second = normed + feed + bias_values[2]
    encoded, final_back = jax.vjp(layer_norm, second, gain_values[1], bias_values[3])
    mask_rows = valid_mask.astype(jnp.float32)
    error = encoded - teacher
    sum_sq, valid_total = lax.psum(
        (jnp.sum(mask_rows[:, None] * error * error), jnp.sum(mask_rows)), ("dp", "tensor")
    )
    loss = sum_sq / (D * valid_total)
    grad_encoded = mask_rows[:, None] * error * (tokens_total / valid_total)
    grad_second, grad_gain_two, grad_shift_two = final_back(grad_encoded)
    second_low = grad_second.astype(jnp.bfloat16)
    fetched = fetch_weights(w_qkv, b_qv, w_out, w_in, b_in, w_back, ln_gains, row_biases)
    qkv_weight, bias_pair, out_weight, in_weight, in_bias, back_weight, gains, biases = fetched
    full_in, full_bias, full_back = widen_units(in_weight, in_bias, back_weight)
    grad_active = jnp.einsum("nd,fd->nf", second_low, full_back, preferred_element_type=jnp.float32)
    grad_inner = gelu_back(grad_active)[0].astype(jnp.bfloat16)
    grad_in_full = jnp.einsum(
        "nd,nf->df", normed_low, grad_inner, preferred_element_type=jnp.float32
    )
    grad_back_full = jnp.einsum("nf,nd->fd", active, second_low, preferred_element_type=jnp.float32)
    grad_bias_full = jnp.sum(grad_inner, axis=0, dtype=jnp.float32).reshape(-1, 64)
    grad_in_weight, grad_in_bias, grad_back_weight = (
        lax.psum_scatter(
            grad_in_full.astype(jnp.bfloat16), "tensor", scatter_dimension=1, tiled=True
        ).astype(jnp.float32),
        lax.psum_scatter(
            grad_bias_full.astype(jnp.bfloat16), "tensor", scatter_dimension=0, tiled=True
        ).astype(jnp.float32),
        lax.psum_scatter(
            grad_back_full.astype(jnp.bfloat16), "tensor", scatter_dimension=0, tiled=True
        ).astype(jnp.float32),
    )
    grad_feed = jnp.einsum("nf,df->nd", grad_inner, full_in, preferred_element_type=jnp.float32)
    grad_normed = grad_second + grad_feed
    grad_mixed, grad_gain_one, grad_shift_one = first_back(grad_normed)
    mixed_low = grad_mixed.astype(jnp.bfloat16)
    whole_grad_mixer = lax.all_gather(mixed_low, "tensor", axis=0, tiled=True)
    grad_context = jnp.einsum(
        "nd,ed->ne", whole_grad_mixer, out_weight, preferred_element_type=jnp.float32
    ).astype(jnp.bfloat16)
    grad_out_weight = jnp.einsum(
        "ne,nd->ed", context, whole_grad_mixer, preferred_element_type=jnp.float32
    )
    grad_items = grad_context.reshape(seq_count, blocks_count, BLK, head_local, HD).transpose(
        0, 3, 1, 2, 4
    )
    grad_items = grad_items.reshape(seq_count * head_local, blocks_count, BLK, HD)
    grad_stack = lax.map(run_backward, (items, chosen_all, grad_items, log_middle, log_edge))
    grad_projected = grad_stack.reshape(seq_count, head_local, 3, blocks_count, BLK, HD).transpose(
        2, 0, 3, 4, 1, 5
    )
    grad_projected = grad_projected.reshape(3, group_rows, head_local * HD)
    grad_bias_pair = jnp.stack(
        [
            jnp.sum(grad_projected[0], axis=0, dtype=jnp.float32),
            jnp.sum(grad_projected[2], axis=0, dtype=jnp.float32),
        ]
    ).reshape(2, head_local, HD)
    grad_qkv_weight = jnp.einsum(
        "nd,kne->kde", whole_in, grad_projected, preferred_element_type=jnp.float32
    )
    piece = grad_projected
    grad_tokens = grad_mixed + lax.psum_scatter(
        jnp.einsum("kne,kde->nd", piece, qkv_weight, preferred_element_type=jnp.float32).astype(
            jnp.bfloat16
        ),
        "tensor",
        scatter_dimension=0,
        tiled=True,
    ).astype(jnp.float32)
    grads = (
        lax.psum_scatter(grad_qkv_weight, "dp", scatter_dimension=1, tiled=True),
        lax.psum_scatter(grad_bias_pair, "dp", scatter_dimension=2, tiled=True),
        lax.psum_scatter(grad_out_weight, "dp", scatter_dimension=1, tiled=True),
        lax.psum_scatter(grad_in_weight, "dp", scatter_dimension=0, tiled=True),
        lax.psum_scatter(grad_in_bias, "dp", scatter_dimension=1, tiled=True),
        lax.psum_scatter(grad_back_weight, "dp", scatter_dimension=1, tiled=True),
    )
    gain_terms = jnp.stack([grad_gain_one, grad_gain_two])
    bias_terms = jnp.stack(
        [jnp.sum(grad_mixed, axis=0), grad_shift_one, jnp.sum(grad_second, axis=0), grad_shift_two]
    )
    vectors = (
        lax.psum_scatter(gain_terms, ("dp", "tensor"), scatter_dimension=1, tiled=True),
        lax.psum_scatter(bias_terms, ("dp", "tensor"), scatter_dimension=1, tiled=True),
    )
    return (
        loss,
        encoded,
        grad_tokens,
        grads[0],
        grads[1],
        grads[2],
        grads[3],
        grads[4],
        grads[5],
        vectors[0],
        vectors[1],
    )


def solution(mesh):
    in_specs = (
        P(("dp", "tensor"), None),
        P(("dp", "tensor"), None),
        P(("dp", "tensor")),
        P(),
        P(None, "dp", "tensor"),
        P(None, "tensor", "dp"),
        P("tensor", "dp"),
        P("dp", "tensor"),
        P("tensor", "dp"),
        P("tensor", "dp"),
        P(None, "dp"),
        P(None, "dp"),
    )
    out_specs = (
        P(),
        P(("dp", "tensor"), None),
        P(("dp", "tensor"), None),
        P(None, "dp", "tensor"),
        P(None, "tensor", "dp"),
        P("tensor", "dp"),
        P("dp", "tensor"),
        P("tensor", "dp"),
        P("tensor", "dp"),
        P(None, ("dp", "tensor")),
        P(None, ("dp", "tensor")),
    )
    return jax.shard_map(
        per_device, mesh=mesh, in_specs=in_specs, out_specs=out_specs, check_vma=False
    )
```

profile of v0, /device:TPU:0, one launch (start us, length us, event | category | flops | bytes accessed | tf_op | source)
XLA Modules:
  0.0 1814.6 jit_solution(15611825318617754182)
XLA Ops:
  10.3 32.2 %all_gather.47 = bf16[2,3,64]{1,0,2:T(2,128)(2,1)S(1)} all-gather(bf16[2,3,8]{1,0,2:T(2,128)(2,1)S(1)} %copy.288), channel_id=1, replica_groups=mesh['dp'=8,'tensor'=4] {'dp'}, dimensions={2}, use_global_device_ids=true | all-gather | bytes 864 | tf_op jit(solution)/shard_map/all_gather | solution.py:32
  44.8 31.3 %all_gather.48 = bf16[192,768]{0,1:T(8,128)(2,1)S(1)} all-gather(bf16[192,96]{0,1:T(8,128)(2,1)S(1)} %copy.293), channel_id=1, replica_groups=mesh['dp'=8,'tensor'=4] {'dp'}, dimensions={1}, use_global_device_ids=true | all-gather | bytes 331776 | tf_op jit(solution)/shard_map/all_gather | solution.py:33
  76.1 42.3 %all_gather.45 = bf16[3,768,192]{2,0,1:T(4,128)(2,1)S(1)} all-gather(bf16[3,96,192]{2,0,1:T(4,128)(2,1)S(1)} %copy.286), channel_id=1, replica_groups=mesh['dp'=8,'tensor'=4] {'dp'}, dimensions={1}, use_global_device_ids=true | all-gather | bytes 995328 | tf_op jit(solution)/shard_map/all_gather | solution.py:31
  118.6 11.4 fusion.110
  130.0 13.8 reshape.654
  143.8 17.0 copy.291
  161.6 175.6 %while.28 = (s32[]{:T(128)}, bf16[6,32,64,64]{3,2,1,0:T(8,128)(2,1)}, f32[6,30,64]{2,1,0:T(8,128)S(1)}, f32[6,128]{1,0:T(8,128)S(1)}, bf16[6,3,32,64,64]{4,2,3,1...) while((s32[]{:T(128)}, ...), condition=%wide.region_5.6_spmd, body=%wide.region_0.5_spmd.sunk | while | flops 380113600 | bytes 35916652 | solution.py:239
  353.1 37.5 %psum.15 = f32[]{:T(128)} all-reduce(f32[]{:T(128)} %convert_reduce_fusion.2), channel_id=1, replica_groups=mesh['dp'=8,'tensor'=4] {'dp','tensor'}, use_global_device_ids=true, to_apply=%region_14.15 | all-reduce | flops 1 | bytes 8 | tf_op jit(solution)/shard_map/psum | solution.py:266
  390.6 20.0 %all-gather.1 = bf16[8,96,2]{1,2,0:T(2,128)(2,1)S(1)} all-gather(bf16[1,96,2]{1,2,0:T(2,128)(2,1)S(1)} %bitcast.468), channel_id=1, replica_groups=mesh['dp'=8,'tensor'=4] {'dp'}, dimensions={0}, use_global_device_ids=true | all-gather | bytes 3456 | tf_op jit(solution)/shard_map/all_gather | solution.py:37
  410.7 16.3 all-gather
  427.1 26.0 %all_gather.53 = bf16[12,64]{0,1:T(8,128)(2,1)S(1)} all-gather(bf16[12,8]{0,1:T(8,128)(2,1)S(1)} %copy-done.28), channel_id=1, replica_groups=mesh['dp'=8,'tensor'=4] {'dp'}, dimensions={1}, use_global_device_ids=true | all-gather | bytes 1728 | tf_op jit(solution)/shard_map/all_gather | solution.py:35
  462.3 11.1 fusion.126
  473.4 13.5 all-gather.18.cloned.1.call-done
  486.9 13.2 fusion.134
  507.9 20.5 %fusion.135 = (bf16[3072]{0:T(1024)(128)(2,1)}, bf16[1024,3072]{1,0:T(8,128)(2,1)}) fusion(bf16[3072,768]{0,1:T(8,128)(2,1)S(1)} %bitcast.472, f32[1024,768]{1,0:T(8,128)S(1)} %get-tuple-element.307, f32[1024]{0:T(1024)S(1)} %negate_multiply_fusion.1, f32[1024,3072]{1,0:T(8,128)} %fusion.126, f32[3072]{0:T(1024)S(1)} %reshape.666), kind=kOutput, calls=%fused_computation.289 | convolution fusion | flops 4915196928 | bytes 26761216 | tf_op jit(solution)/shard_map/nd,fd->nf/dot_general | solution.py:276
  528.5 8.9 multiply_reduce_fusion.3
  542.3 13.4 convolution_convert_fusion.6
  555.7 10.3 convolution_convert_fusion.7
  566.0 22.7 %all-gather.20.cloned.1.call-done = bf16[4096,768]{1,0:T(8,128)(2,1)} async-done(((bf16[1024,768]{1,0:T(8,128)(2,1)}), bf16[4096,768]{1,0:T(8,128)(2,1)}) %all-gather.20.cloned.1.call-update) | async-done | bytes 6291472 | tf_op jit(solution)/shard_map/all_gather | solution.py:298
  610.3 881.7 %while.29 = (s32[]{:T(128)}, bf16[6,3,32,64,64]{4,3,2,1,0:T(8,128)(2,1)}, bf16[6,3,32,64,64]{4,2,3,1,0:T(8,128)(2,1)}, f32[6,128]{1,0:T(8,128)S(1)}, bf16[6,32,6...) while((s32[]{:T(128)}, ...), condition=%wide.region_26.27_spmd, body=%wide.region_19.26_spmd.sunk | while | flops 1145694464 | bytes 190884928 | solution.py:309
  650.9 7.4 fusion.261
  686.3 16.3 slice_reduce_fusion.12
  729.1 16.4 slice_reduce_fusion.13
  793.2 7.3 fusion.261
  828.5 16.3 slice_reduce_fusion.12
  871.2 16.4 slice_reduce_fusion.13
  935.3 7.3 fusion.261
  970.6 16.3 slice_reduce_fusion.12
  1013.3 16.4 slice_reduce_fusion.13
  1077.3 7.3 fusion.261
  1112.6 16.3 slice_reduce_fusion.12
  1155.3 16.4 slice_reduce_fusion.13
  1219.4 7.3 fusion.261
  1254.7 16.3 slice_reduce_fusion.12
  1297.4 16.4 slice_reduce_fusion.13
  1361.5 7.3 fusion.261
  1396.7 16.3 slice_reduce_fusion.12
  1439.4 16.4 slice_reduce_fusion.13
  1492.0 13.5 copy.298
  1505.5 13.1 reshape.661
  1518.6 7.5 fusion.118
  1533.8 9.6 bitcast_convert_fusion
  1552.6 7.8 fusion
  1568.7 37.2 %all-reduce.13 = (f32[2,3,64]{2,1,0:T(4,128)S(1)}, f32[12,64]{1,0:T(8,128)S(1)}) all-reduce(f32[2,3,64]{2,1,0:T(4,128)S(1)} %pad_maximum_fusion.13, f32[12,64]{1,0:T(8,128)S(1)} %dynamic-slice_convert_fusion.2), channel_id=5, replica_groups=mesh['dp'=8,'tensor'=4] {'dp'}, use_global_device_ids=true, to_apply=%region_31.32.clone | all-reduce | flops 1152 | bytes 9216
  1610.9 50.1 %reduce-scatter.23.cloned.1.call-done = bf16[1024,768]{1,0:T(8,128)(2,1)} async-done(((bf16[4096,768]{1,0:T(8,128)(2,1)}), bf16[1024,768]{1,0:T(8,128)(2,1)}) %reduce-scatter.23.cloned.1.call-update) | async-done | bytes 1572880 | tf_op jit(solution)/shard_map/reduce_scatter | solution.py:324
  1665.5 40.4 %all-reduce.12 = (f32[]{:T(128)}, f32[2,768]{1,0:T(2,128)S(1)}, f32[4,768]{1,0:T(4,128)S(1)}) all-reduce(f32[]{:T(128)} %get-tuple-element.263, f32[2,768]{1,0:T(2,128)S(1)} %pad_maximum_fusion.11, f32[4,768]{1,0:T(4,128)S(1)} %pad_maximum_fusion.10), channel_id=1, replica_groups=mesh['dp'=8,'tensor'=4] {'dp','tensor'}, use_global_device_ids=true, to_apply=%region_12.13 | all-reduce | flops 4609 | bytes 36872 | tf_op jit(solution)/shard_map/psum | solution.py:266
  1707.9 26.9 %reduce-scatter.35.cloned.1.call-done = f32[96,768]{1,0:T(8,128)} async-done(((f32[768,768]{1,0:T(8,128)}), f32[96,768]{1,0:T(8,128)}) %reduce-scatter.35.cloned.1.call-update) | async-done | bytes 294928
  1734.8 72.0 %reduce-scatter.27.cloned.1.call-done = f32[96,768]{1,0:T(8,128)} async-done(((f32[768,768]{1,0:T(8,128)}), f32[96,768]{1,0:T(8,128)}) %reduce-scatter.27.cloned.1.call-update) | async-done | bytes 294928 | tf_op jit(solution)/shard_map/reduce_scatter | solution.py:336
  (854 shorter events, 883.9 us)
Async XLA Ops:
  7.2 111.4 %copy-start = (s32[12,32,3,32]{3,1,2,0:T(8,128)S(1)}, s32[12,32,3,32]{3,1,2,0:T(8,128)}, u32[]{:S(2)}) copy-start(s32[12,32,3,32]{3,1,2,0:T(8,128)} %param.19) | copy-start | bytes 442372
  7.2 111.4 %all-gather.10.cloned.1.call-start = ((), (), s32[]{:S(2)}) async-start(), calls=%async_computation.8 | async-start | bytes 7864320 | tf_op jit(solution)/shard_map/all_gather | solution.py:229
  7.9 343.5 %all-gather.12.cloned.1.call-start = ((), (), s32[]{:S(2)}) async-start(), calls=%async_computation.10 | async-start | bytes 1327104 | tf_op jit(solution)/shard_map/all_gather | solution.py:34
  8.7 343.3 %all-gather.16.cloned.1.call-start = ((), (), s32[]{:S(2)}) async-start(), calls=%async_computation.12 | async-start | bytes 1327104 | tf_op jit(solution)/shard_map/all_gather | solution.py:36
  9.4 449.8 %reduce-scatter.21.cloned.1.call-start = ((), (), s32[]{:S(2)}) async-start(), calls=%async_computation.9 | async-start | bytes 7864320 | tf_op jit(solution)/shard_map/reduce_scatter | solution.py:245
  118.5 11.6 copy-start.16
  351.3 39.3 %copy-start.30 = (bf16[2,96]{1,0:T(2,128)(2,1)S(1)}, bf16[2,96]{1,0:T(2,128)(2,1)}, u32[]{:S(2)}) copy-start(bf16[2,96]{1,0:T(2,128)(2,1)} %param.26) | copy-start | bytes 1156
  351.3 59.5 %copy-start.29 = (bf16[4,96]{1,0:T(4,128)(2,1)S(1)}, bf16[4,96]{1,0:T(4,128)(2,1)}, u32[]{:S(2)}) copy-start(bf16[4,96]{1,0:T(4,128)(2,1)} %param.27) | copy-start | bytes 2308
  351.3 75.8 %copy-start.28 = (bf16[12,8]{0,1:T(8,128)(2,1)S(1)}, bf16[12,8]{0,1:T(8,128)(2,1)}, u32[]{:S(2)}) copy-start(bf16[12,8]{0,1:T(8,128)(2,1)} %param.24) | copy-start | bytes 580
  351.3 107.9 %copy-start.9 = (bf16[1024,768]{1,0:T(8,128)(2,1)S(1)}, bf16[1024,768]{1,0:T(8,128)(2,1)}, u32[]{:S(2)}) copy-start(bf16[1024,768]{1,0:T(8,128)(2,1)} %param.16) | copy-start | bytes 4718596
  351.3 111.0 %all-gather.14.cloned.1.call-start = ((), (), s32[]{:S(2)}) async-start(), calls=%async_computation.11 | async-start | bytes 5898240 | tf_op jit(solution)/shard_map/all_gather | solution.py:44
  351.9 135.0 %all-gather.18.cloned.1.call-start = ((), (), s32[]{:S(2)}) async-start(), calls=%async_computation.13 | async-start | bytes 5898240 | tf_op jit(solution)/shard_map/all_gather | solution.py:46
  352.5 236.3 %all-gather.20.cloned.1.call-start = ((), (), s32[]{:S(2)}) async-start(), calls=%async_computation.14 | async-start | bytes 7864320 | tf_op jit(solution)/shard_map/all_gather | solution.py:298
  506.2 22.3 %slice-start = ((s8[4718592]{0:T(1024)(128)(4,1)}), s8[524288]{0:T(1024)(128)(4,1)S(1)}, s32[]{:S(2)}) async-start(s8[4718592]{0:T(1024)(128)(4,1)} %bitcast.469), calls=%async_computation.22 | async-start | bytes 1048576
  507.8 20.6 %copy-start.12 = (f32[1024,768]{1,0:T(8,128)}, f32[1024,768]{1,0:T(8,128)S(1)}, u32[]{:S(2)}) copy-start(f32[1024,768]{1,0:T(8,128)S(1)} %get-tuple-element.307) | copy-start | bytes 9437188
  507.9 34.4 %copy-start.22 = (f32[1024]{0:T(1024)}, f32[1024]{0:T(1024)S(1)}, u32[]{:S(2)}) copy-start(f32[1024]{0:T(1024)S(1)} %negate_multiply_fusion.1) | copy-start | bytes 12292
  507.9 20.6 %copy-start.11 = (bf16[1024,768]{1,0:T(8,128)(2,1)S(1)}, bf16[1024,768]{1,0:T(8,128)(2,1)}, u32[]{:S(2)}) copy-start(bf16[1024,768]{1,0:T(8,128)(2,1)} %reduce-scatter.21.cloned.1.call-done) | copy-start | bytes 4718596
  507.9 20.6 %slice-start.1 = ((s8[4718592]{0:T(1024)(128)(4,1)}), s8[4194304]{0:T(1024)(128)(4,1)S(1)}, s32[]{:S(2)}) async-start(s8[4718592]{0:T(1024)(128)(4,1)} %bitcast.469), calls=%async_computation.23 | async-start | bytes 8388608
  539.2 16.4 copy-start.18
  542.2 1001.3 %reduce-scatter.29.cloned.1.call-start = ((), (), s32[]{:S(2)}) async-start(), calls=%async_computation.18 | async-start | bytes 5898240 | tf_op jit(solution)/shard_map/reduce_scatter | solution.py:290
  555.6 990.8 %reduce-scatter.25.cloned.1.call-start = ((), (), s32[]{:S(2)}) async-start(), calls=%async_computation.16 | async-start | bytes 5898240 | tf_op jit(solution)/shard_map/reduce_scatter | solution.py:284
  566.0 1041.4 %reduce-scatter.33.cloned.1.call-start = ((), (), s32[]{:S(2)}) async-start(), calls=%async_computation.20 | async-start | bytes 884736
  610.3 998.8 %reduce-scatter.31.cloned.1.call-start = ((), (), s32[]{:S(2)}) async-start(), calls=%async_computation.19 | async-start | bytes 2211840
  686.3 16.3 copy-start.2
  710.4 10.3 copy-start.6
  729.1 16.4 copy-start.3
  828.5 16.3 copy-start.2
  852.5 10.2 copy-start.6
  871.2 16.4 copy-start.3
  970.5 16.3 copy-start.2
  994.6 10.2 copy-start.6
  1013.3 16.4 copy-start.3
  1112.6 16.3 copy-start.2
  1136.6 10.2 copy-start.6
  1155.3 16.4 copy-start.3
  1254.7 16.3 copy-start.2
  1297.4 16.4 copy-start.3
  1396.7 16.3 copy-start.2
  1439.4 16.4 copy-start.3
  1533.8 127.2 %reduce-scatter.23.cloned.1.call-start = ((), (), s32[]{:S(2)}) async-start(), calls=%async_computation.15 | async-start | bytes 7864320 | tf_op jit(solution)/shard_map/reduce_scatter | solution.py:324
  1543.5 191.3 %reduce-scatter.35.cloned.1.call-start = ((), (), s32[]{:S(2)}) async-start(), calls=%async_computation.21 | async-start | bytes 2654208
  1546.3 15.5 copy-start.23
  1546.3 17.7 copy-start.20
  1546.3 17.7 copy-start.26
  1546.3 260.4 %reduce-scatter.27.cloned.1.call-start = ((), (), s32[]{:S(2)}) async-start(), calls=%async_computation.17 | async-start | bytes 2654208 | tf_op jit(solution)/shard_map/reduce_scatter | solution.py:336
  1560.5 3.6 collective-permute-start
  1564.3 96.7 %copy-start.19 = (f32[1024]{0:T(1024)S(1)}, f32[1024]{0:T(1024)}, u32[]{:S(2)}) copy-start(f32[1024]{0:T(1024)} %copy-done.18) | copy-start | bytes 12292
  1610.2 196.6 %copy-start.1 = (s32[12,32,3,32]{3,1,2,0:T(8,128)S(1)}, s32[12,32,3,32]{3,1,2,0:T(8,128)}, u32[]{:S(2)}) copy-start(s32[12,32,3,32]{3,1,2,0:T(8,128)} %param.19) | copy-start | bytes 442372
  (34 other events, 147.1 us)
Sparse Core Ops, SparseCore 0:
  9.6 49.0 all-gather.9
  60.9 50.5 all-gather.11
  113.6 40.8 all-gather.15
  351.4 57.4 reduce-scatter.20
  410.4 37.4 all-gather.13
  449.4 37.4 all-gather.17
  542.3 46.3 all-gather.19
  591.4 47.8 reduce-scatter.28
  641.9 47.8 reduce-scatter.24
  693.2 62.4 reduce-scatter.32
  1533.9 67.1 reduce-scatter.30
  1603.6 57.3 reduce-scatter.22
  1665.1 69.6 reduce-scatter.34
  1738.7 67.9 reduce-scatter.26
where the time goes:
time: 1830 us; the launch traced here: 1810 us
  local copies, waits for them, and re-layouts  596 us (33%)
  matrix products  389 us (21%)
  blocking collectives  296 us (16%)
  other arithmetic  291 us (16%)
  waiting for transfers between devices  188 us (10%)
  loops' own time  32 us (2%)
  between operations  19.2 us (1%)
    while x216, local copies, waits for them, and re-layouts  240 us
    reduce_sum x12, other arithmetic, spread_slots(): jnp.sum(parts_grad[:, 3], axis=0)[None]  196 us
    reshape x12, local copies, waits for them, and re-layouts, spread_slots(): parts_grad = slot_grads.reshape(middle, -1, BLK, slot_grads.shape[-1])  80 us
    psum x2, blocking collectives, per_device(): lax.psum((jnp.sum(mask_rows[:, None] * error * error), jnp.sum(mask_rows)...  77.9 us
    reduce_scatter x1, waiting for transfers between devices, per_device(): lax.psum_scatter(grad_in_weight, 'dp', scatter_dimension=0, tiled=True)  72 us
    reduce_scatter x1, waiting for transfers between devices, per_device(): lax.psum_scatter(jnp.einsum('kne,kde->nd', piece, qkv_weight, preferred_e...  50.1 us
    dot_general x12, matrix products, middle_scores(): jnp.einsum('mqd,mkd->mqk', mid_queries, key_slots, preferred_element_type...  47.5 us
    unnamed x2, blocking collectives  45.1 us
  transfers between devices with their start and end apart: 15, of which 5 were waited for; matrix products, arithmetic and copies ran while one was open for 67% of the time, Pallas kernels for 0%

commit v1 on v0

--- a/solution.py
+++ b/solution.py
@@ -12,6 +12,28 @@
 exact_precision = lax.Precision.HIGHEST
 
 
+def joined_along(blocks, dim):
+    blocks = jnp.moveaxis(blocks, 0, dim)
+    shape = blocks.shape
+    return blocks.reshape(*shape[:dim], shape[dim] * shape[dim + 1], *shape[dim + 2 :])
+
+
+def collected_by_bits(x, axis):
+    size = lax.axis_size(axis)
+    tiles = x[None]
+    for level in range(size.bit_length() - 1):
+        apart = 1 << level
+        received = lax.ppermute(tiles, axis, [(i, i ^ apart) for i in range(size)])
+        both = jnp.stack([tiles, received])
+        upper = lax.axis_index(axis) >> level & 1
+        tiles = jnp.where(upper == 0, both, both[::-1]).reshape(-1, *x.shape)
+    return tiles
+
+
+def gather_by_bits(x, axis, dim):
+    return joined_along(collected_by_bits(x, axis), dim)
+
+
 def layer_norm(values, gain, shift):
     centred = values - jnp.mean(values, axis=-1, keepdims=True)
     variance = jnp.mean(centred * centred, axis=-1, keepdims=True)
@@ -28,7 +50,7 @@
 
 def fetch_weights(w_qkv, b_qv, w_out, w_in, b_in, w_back, ln_gains, row_biases):
     return (
-        lax.all_gather(w_qkv, "dp", axis=1, tiled=True),
+        gather_by_bits(w_qkv, "dp", 1),
         lax.all_gather(b_qv, "dp", axis=2, tiled=True),
         lax.all_gather(w_out, "dp", axis=1, tiled=True),
         lax.all_gather(w_in, "dp", axis=0, tiled=True),

time: 1830 us -> 1820 us (level)
  blocking collectives: 296 us -> 265 us
    all_gather x1 -> x0, blocking collectives: 42.3 us -> none  [fetch_weights(): lax.all_gather(w_qkv, 'dp', axis=1, tiled=True)]
  transfers between devices with their start and end apart: 15 -> 18, of which waited for: 5 -> 6; matrix products, arithmetic and copies ran while one was open for 67% -> 68% of each run, Pallas kernels for 0% -> 0%
where the time goes in v1:
time: 1820 us; the launch traced here: 1800 us
  local copies, waits for them, and re-layouts  603 us (33%)
  matrix products  386 us (21%)
  other arithmetic  297 us (16%)
  blocking collectives  265 us (15%)
  waiting for transfers between devices  195 us (11%)
  loops' own time  31.9 us (2%)
  between operations  19.3 us (1%)
    while x216, local copies, waits for them, and re-layouts  241 us
    reduce_sum x12, other arithmetic, spread_slots(): jnp.sum(parts_grad[:, 3], axis=0)[None]  197 us
    reshape x12, local copies, waits for them, and re-layouts, spread_slots(): parts_grad = slot_grads.reshape(middle, -1, BLK, slot_grads.shape[-1])  80 us
    psum x2, blocking collectives, per_device(): lax.psum((jnp.sum(mask_rows[:, None] * error * error), jnp.sum(mask_rows)...  78.2 us
    reduce_scatter x1, waiting for transfers between devices, per_device(): lax.psum_scatter(grad_in_weight, 'dp', scatter_dimension=0, tiled=True)  72 us
    reduce_scatter x1, waiting for transfers between devices, per_device(): lax.psum_scatter(jnp.einsum('kne,kde->nd', piece, qkv_weight, preferred_e...  50.6 us
    dot_general x12, matrix products, middle_scores(): jnp.einsum('mqd,mkd->mqk', mid_queries, key_slots, preferred_element_type...  47.5 us
    unnamed x2, blocking collectives  44.7 us
  transfers between devices with their start and end apart: 18, of which 6 were waited for; matrix products, arithmetic and copies ran while one was open for 68% of the time, Pallas kernels for 0%

profile of v1, /device:TPU:0, one launch (start us, length us, event | category | flops | bytes accessed | tf_op | source)
XLA Modules:
  0.0 1801.9 jit_solution(16670056493569481237)
XLA Ops:
  12.6 30.8 %all_gather.42 = bf16[2,3,64]{1,0,2:T(2,128)(2,1)S(1)} all-gather(bf16[2,3,8]{1,0,2:T(2,128)(2,1)S(1)} %copy.280), channel_id=1, replica_groups=mesh['dp'=8,'tensor'=4] {'dp'}, dimensions={2}, use_global_device_ids=true | all-gather | bytes 864 | tf_op jit(solution)/shard_map/all_gather | solution.py:54
  45.9 7.9 collective-permute-done.1
  54.1 43.6 %all_gather.43 = bf16[192,768]{0,1:T(8,128)(2,1)S(1)} all-gather(bf16[192,96]{0,1:T(8,128)(2,1)S(1)} %copy.285), channel_id=1, replica_groups=mesh['dp'=8,'tensor'=4] {'dp'}, dimensions={1}, use_global_device_ids=true | all-gather | bytes 331776 | tf_op jit(solution)/shard_map/all_gather | solution.py:55
  100.7 8.6 fusion.110
  109.3 13.8 reshape.674
  123.1 16.9 copy.283
  140.8 179.1 %while.28 = (s32[]{:T(128)}, bf16[6,32,64,64]{3,2,1,0:T(8,128)(2,1)}, f32[6,30,64]{2,1,0:T(8,128)}, f32[6,128]{1,0:T(8,128)S(1)}, bf16[6,3,32,64,64]{4,2,3,1,0:T...) while((s32[]{:T(128)}, ...), condition=%wide.region_5.6_spmd, body=%wide.region_0.5_spmd.sunk | while | flops 380113600 | bytes 35890540 | solution.py:261
  335.8 37.6 %psum.15 = f32[]{:T(128)} all-reduce(f32[]{:T(128)} %convert_reduce_fusion.2), channel_id=1, replica_groups=mesh['dp'=8,'tensor'=4] {'dp','tensor'}, use_global_device_ids=true, to_apply=%region_14.15 | all-reduce | flops 1 | bytes 8 | tf_op jit(solution)/shard_map/psum | solution.py:288
  373.4 19.9 %all-gather.1 = bf16[8,96,2]{1,2,0:T(2,128)(2,1)S(1)} all-gather(bf16[1,96,2]{1,2,0:T(2,128)(2,1)S(1)} %bitcast.496), channel_id=1, replica_groups=mesh['dp'=8,'tensor'=4] {'dp'}, dimensions={0}, use_global_device_ids=true | all-gather | bytes 3456 | tf_op jit(solution)/shard_map/all_gather | solution.py:59
  393.4 16.3 all-gather
  409.8 26.0 %all_gather.48 = bf16[12,64]{0,1:T(8,128)(2,1)S(1)} all-gather(bf16[12,8]{0,1:T(8,128)(2,1)S(1)} %copy-done.28), channel_id=1, replica_groups=mesh['dp'=8,'tensor'=4] {'dp'}, dimensions={1}, use_global_device_ids=true | all-gather | bytes 1728 | tf_op jit(solution)/shard_map/all_gather | solution.py:57
  445.0 11.2 fusion.126
  456.2 12.6 all-gather.18.cloned.1.call-done
  468.7 13.1 fusion.134
  489.7 20.6 %fusion.135 = (bf16[3072]{0:T(1024)(128)(2,1)}, bf16[1024,3072]{1,0:T(8,128)(2,1)}) fusion(bf16[3072,768]{0,1:T(8,128)(2,1)S(1)} %bitcast.500, f32[1024,768]{1,0:T(8,128)S(1)} %get-tuple-element.307, f32[1024]{0:T(1024)S(1)} %negate_multiply_fusion.1, f32[1024,3072]{1,0:T(8,128)} %fusion.126, f32[3072]{0:T(1024)S(1)} %reshape.686), kind=kOutput, calls=%fused_computation.295 | convolution fusion | flops 4915196928 | bytes 26761216 | tf_op jit(solution)/shard_map/nd,fd->nf/dot_general | solution.py:298
  510.3 8.9 multiply_reduce_fusion.3
  524.1 13.4 convolution_convert_fusion.6
  537.6 10.2 convolution_convert_fusion.7
  547.9 22.6 %all-gather.20.cloned.1.call-done = bf16[4096,768]{1,0:T(8,128)(2,1)} async-done(((bf16[1024,768]{1,0:T(8,128)(2,1)}), bf16[4096,768]{1,0:T(8,128)(2,1)}) %all-gather.20.cloned.1.call-update) | async-done | bytes 6291472 | tf_op jit(solution)/shard_map/all_gather | solution.py:320
  592.2 887.4 %while.29 = (s32[]{:T(128)}, bf16[6,3,32,64,64]{4,3,2,1,0:T(8,128)(2,1)}, bf16[6,3,32,64,64]{4,2,3,1,0:T(8,128)(2,1)}, f32[6,128]{1,0:T(8,128)S(1)}, bf16[6,32,6...) while((s32[]{:T(128)}, ...), condition=%wide.region_26.27_spmd, body=%wide.region_19.26_spmd.sunk | while | flops 1145694464 | bytes 190884928 | solution.py:331
  633.6 7.3 fusion.263
  669.1 16.3 slice_reduce_fusion.12
  712.1 16.5 slice_reduce_fusion.13
  776.8 7.3 fusion.263
  812.2 16.3 slice_reduce_fusion.12
  855.1 16.5 slice_reduce_fusion.13
  919.9 7.3 fusion.263
  955.3 16.3 slice_reduce_fusion.12
  998.1 16.5 slice_reduce_fusion.13
  1062.9 7.3 fusion.263
  1098.2 16.3 slice_reduce_fusion.12
  1141.1 16.5 slice_reduce_fusion.13
  1205.9 7.3 fusion.263
  1241.3 16.3 slice_reduce_fusion.12
  1284.1 16.5 slice_reduce_fusion.13
  1348.9 7.3 fusion.263
  1384.3 16.3 slice_reduce_fusion.12
  1427.1 16.5 slice_reduce_fusion.13
  1479.6 13.6 copy.290
  1493.1 13.1 reshape.681
  1506.2 7.5 fusion.118
  1521.4 9.5 bitcast_convert_fusion
  1540.0 7.8 fusion
  1556.1 36.9 %all-reduce.13 = (f32[2,3,64]{2,1,0:T(4,128)S(1)}, f32[12,64]{1,0:T(8,128)S(1)}) all-reduce(f32[2,3,64]{2,1,0:T(4,128)S(1)} %pad_maximum_fusion.16, f32[12,64]{1,0:T(8,128)S(1)} %dynamic-slice_convert_fusion.2), channel_id=5, replica_groups=mesh['dp'=8,'tensor'=4] {'dp'}, use_global_device_ids=true, to_apply=%region_31.32.clone | all-reduce | flops 1152 | bytes 9216
  1598.0 50.6 %reduce-scatter.23.cloned.1.call-done = bf16[1024,768]{1,0:T(8,128)(2,1)} async-done(((bf16[4096,768]{1,0:T(8,128)(2,1)}), bf16[1024,768]{1,0:T(8,128)(2,1)}) %reduce-scatter.23.cloned.1.call-update) | async-done | bytes 1572880 | tf_op jit(solution)/shard_map/reduce_scatter | solution.py:346
  1653.1 40.6 %all-reduce.12 = (f32[]{:T(128)}, f32[2,768]{1,0:T(2,128)S(1)}, f32[4,768]{1,0:T(4,128)S(1)}) all-reduce(f32[]{:T(128)} %get-tuple-element.263, f32[2,768]{1,0:T(2,128)S(1)} %pad_maximum_fusion.14, f32[4,768]{1,0:T(4,128)S(1)} %pad_maximum_fusion.13), channel_id=1, replica_groups=mesh['dp'=8,'tensor'=4] {'dp','tensor'}, use_global_device_ids=true, to_apply=%region_12.13 | all-reduce | flops 4609 | bytes 36872 | tf_op jit(solution)/shard_map/psum | solution.py:288
  1695.6 26.4 %reduce-scatter.35.cloned.1.call-done = f32[96,768]{1,0:T(8,128)} async-done(((f32[768,768]{1,0:T(8,128)}), f32[96,768]{1,0:T(8,128)}) %reduce-scatter.35.cloned.1.call-update) | async-done | bytes 294928
  1722.0 72.0 %reduce-scatter.27.cloned.1.call-done = f32[96,768]{1,0:T(8,128)} async-done(((f32[768,768]{1,0:T(8,128)}), f32[96,768]{1,0:T(8,128)}) %reduce-scatter.27.cloned.1.call-update) | async-done | bytes 294928 | tf_op jit(solution)/shard_map/reduce_scatter | solution.py:358
  (866 shorter events, 898.4 us)
Async XLA Ops:
  7.2 46.9 %copy-start = (s32[12,32,3,32]{3,1,2,0:T(8,128)S(1)}, s32[12,32,3,32]{3,1,2,0:T(8,128)}, u32[]{:S(2)}) copy-start(s32[12,32,3,32]{3,1,2,0:T(8,128)} %param.19) | copy-start | bytes 442372
  7.2 93.5 %all-gather.10.cloned.1.call-start = ((), (), s32[]{:S(2)}) async-start(), calls=%async_computation.8 | async-start | bytes 7864320 | tf_op jit(solution)/shard_map/all_gather | solution.py:251
  7.9 326.2 %all-gather.12.cloned.1.call-start = ((), (), s32[]{:S(2)}) async-start(), calls=%async_computation.10 | async-start | bytes 1327104 | tf_op jit(solution)/shard_map/all_gather | solution.py:56
  8.7 326.0 %all-gather.16.cloned.1.call-start = ((), (), s32[]{:S(2)}) async-start(), calls=%async_computation.12 | async-start | bytes 1327104 | tf_op jit(solution)/shard_map/all_gather | solution.py:58
  8.7 34.7 %collective-permute-start = (bf16[1,3,96,192]{3,2,1,0:T(8,128)(2,1)}, bf16[1,3,96,192]{3,2,1,0:T(8,128)(2,1)S(1)}, u32[]{:S(2)}, u32[]{:S(2)}) collective-permute-start(bf16[1,3,96,192]{3,2,1,0:T(8,128)(2,1)} %bitcast.485), channel_id=1, source_target_pairs={{0,4},{4,0},{8,12},{12,8},{16,20},{20,16},{24,28},{28,24},{1,5},{5... | collective-permute-start | bytes 331784 | tf_op jit(solution)/shard_map/ppermute | solution.py:26
  11.8 430.2 %reduce-scatter.21.cloned.1.call-start = ((), (), s32[]{:S(2)}) async-start(), calls=%async_computation.9 | async-start | bytes 7864320 | tf_op jit(solution)/shard_map/reduce_scatter | solution.py:267
  44.5 9.3 collective-permute-start.1
  54.0 43.7 %collective-permute-start.2 = (bf16[4,3,96,192]{3,2,1,0:T(8,128)(2,1)S(1)}, bf16[4,3,96,192]{3,2,1,0:T(8,128)(2,1)S(1)}, u32[]{:S(2)}, u32[]{:S(2)}) collective-permute-start(bf16[4,3,96,192]{3,2,1,0:T(8,128)(2,1)S(1)} %bitcast.479), channel_id=1, source_target_pairs={{0,16},{4,20},{8,24},{12,28},{16,0},{20,4},{24,8},{28,12},{1,17},{... | collective-permute-start | bytes 1327112 | tf_op jit(solution)/shard_map/ppermute | solution.py:26
  334.0 39.5 %copy-start.30 = (bf16[2,96]{1,0:T(2,128)(2,1)S(1)}, bf16[2,96]{1,0:T(2,128)(2,1)}, u32[]{:S(2)}) copy-start(bf16[2,96]{1,0:T(2,128)(2,1)} %param.26) | copy-start | bytes 1156
  334.0 59.5 %copy-start.29 = (bf16[4,96]{1,0:T(4,128)(2,1)S(1)}, bf16[4,96]{1,0:T(4,128)(2,1)}, u32[]{:S(2)}) copy-start(bf16[4,96]{1,0:T(4,128)(2,1)} %param.27) | copy-start | bytes 2308
  334.0 75.8 %copy-start.28 = (bf16[12,8]{0,1:T(8,128)(2,1)S(1)}, bf16[12,8]{0,1:T(8,128)(2,1)}, u32[]{:S(2)}) copy-start(bf16[12,8]{0,1:T(8,128)(2,1)} %param.24) | copy-start | bytes 580
  334.0 108.0 %copy-start.9 = (bf16[1024,768]{1,0:T(8,128)(2,1)S(1)}, bf16[1024,768]{1,0:T(8,128)(2,1)}, u32[]{:S(2)}) copy-start(bf16[1024,768]{1,0:T(8,128)(2,1)} %param.16) | copy-start | bytes 4718596
  334.0 111.0 %all-gather.14.cloned.1.call-start = ((), (), s32[]{:S(2)}) async-start(), calls=%async_computation.11 | async-start | bytes 5898240 | tf_op jit(solution)/shard_map/all_gather | solution.py:66
  334.6 134.1 %all-gather.18.cloned.1.call-start = ((), (), s32[]{:S(2)}) async-start(), calls=%async_computation.13 | async-start | bytes 5898240 | tf_op jit(solution)/shard_map/all_gather | solution.py:68
  335.2 235.4 %all-gather.20.cloned.1.call-start = ((), (), s32[]{:S(2)}) async-start(), calls=%async_computation.14 | async-start | bytes 7864320 | tf_op jit(solution)/shard_map/all_gather | solution.py:320
  487.9 22.4 %slice-start = ((s8[4718592]{0:T(1024)(128)(4,1)}), s8[524288]{0:T(1024)(128)(4,1)S(1)}, s32[]{:S(2)}) async-start(s8[4718592]{0:T(1024)(128)(4,1)} %bitcast.497), calls=%async_computation.22 | async-start | bytes 1048576
  489.6 20.7 %copy-start.12 = (f32[1024,768]{1,0:T(8,128)}, f32[1024,768]{1,0:T(8,128)S(1)}, u32[]{:S(2)}) copy-start(f32[1024,768]{1,0:T(8,128)S(1)} %get-tuple-element.307) | copy-start | bytes 9437188
  489.6 34.5 %copy-start.22 = (f32[1024]{0:T(1024)}, f32[1024]{0:T(1024)S(1)}, u32[]{:S(2)}) copy-start(f32[1024]{0:T(1024)S(1)} %negate_multiply_fusion.1) | copy-start | bytes 12292
  489.7 20.6 %copy-start.11 = (bf16[1024,768]{1,0:T(8,128)(2,1)S(1)}, bf16[1024,768]{1,0:T(8,128)(2,1)}, u32[]{:S(2)}) copy-start(bf16[1024,768]{1,0:T(8,128)(2,1)} %reduce-scatter.21.cloned.1.call-done) | copy-start | bytes 4718596
  489.7 20.6 %slice-start.1 = ((s8[4718592]{0:T(1024)(128)(4,1)}), s8[4194304]{0:T(1024)(128)(4,1)S(1)}, s32[]{:S(2)}) async-start(s8[4718592]{0:T(1024)(128)(4,1)} %bitcast.497), calls=%async_computation.23 | async-start | bytes 8388608
  521.0 16.5 copy-start.18
  524.0 1006.9 %reduce-scatter.29.cloned.1.call-start = ((), (), s32[]{:S(2)}) async-start(), calls=%async_computation.18 | async-start | bytes 5898240 | tf_op jit(solution)/shard_map/reduce_scatter | solution.py:312
  537.6 996.3 %reduce-scatter.25.cloned.1.call-start = ((), (), s32[]{:S(2)}) async-start(), calls=%async_computation.16 | async-start | bytes 5898240 | tf_op jit(solution)/shard_map/reduce_scatter | solution.py:306
  547.9 1046.5 %reduce-scatter.33.cloned.1.call-start = ((), (), s32[]{:S(2)}) async-start(), calls=%async_computation.20 | async-start | bytes 884736
  592.1 1003.9 %reduce-scatter.31.cloned.1.call-start = ((), (), s32[]{:S(2)}) async-start(), calls=%async_computation.19 | async-start | bytes 2211840
  669.1 16.3 copy-start.2
  693.2 10.3 copy-start.6
  712.1 16.5 copy-start.3
  812.2 16.3 copy-start.2
  855.1 16.5 copy-start.3
  955.3 16.3 copy-start.2
  998.1 16.5 copy-start.3
  1098.2 16.3 copy-start.2
  1141.1 16.5 copy-start.3
  1241.3 16.3 copy-start.2
  1265.4 10.2 copy-start.6
  1284.1 16.5 copy-start.3
  1384.3 16.3 copy-start.2
  1427.1 16.5 copy-start.3
  1521.3 127.2 %reduce-scatter.23.cloned.1.call-start = ((), (), s32[]{:S(2)}) async-start(), calls=%async_computation.15 | async-start | bytes 7864320 | tf_op jit(solution)/shard_map/reduce_scatter | solution.py:346
  1530.9 191.1 %reduce-scatter.35.cloned.1.call-start = ((), (), s32[]{:S(2)}) async-start(), calls=%async_computation.21 | async-start | bytes 2654208
  1533.7 15.4 copy-start.23
  1533.8 17.6 copy-start.20
  1533.8 17.7 copy-start.26
  1533.8 260.2 %reduce-scatter.27.cloned.1.call-start = ((), (), s32[]{:S(2)}) async-start(), calls=%async_computation.17 | async-start | bytes 2654208 | tf_op jit(solution)/shard_map/reduce_scatter | solution.py:358
  1547.9 3.6 collective-permute-start.3
  1551.7 96.9 %copy-start.19 = (f32[1024]{0:T(1024)S(1)}, f32[1024]{0:T(1024)}, u32[]{:S(2)}) copy-start(f32[1024]{0:T(1024)} %copy-done.18) | copy-start | bytes 12292
  1597.2 196.8 %copy-start.1 = (s32[12,32,3,32]{3,1,2,0:T(8,128)S(1)}, s32[12,32,3,32]{3,1,2,0:T(8,128)}, u32[]{:S(2)}) copy-start(s32[12,32,3,32]{3,1,2,0:T(8,128)} %param.19) | copy-start | bytes 442372
  (37 other events, 176.5 us)
Sparse Core Ops, SparseCore 0:
  9.6 49.0 all-gather.9
  60.9 43.0 all-gather.11
  106.2 40.3 all-gather.15
  334.1 56.5 reduce-scatter.20
  392.2 37.4 all-gather.13
  431.2 37.4 all-gather.17
  524.2 46.3 all-gather.19
  573.3 47.8 reduce-scatter.28
  623.7 47.8 reduce-scatter.24
  675.0 62.4 reduce-scatter.32
  1521.5 67.0 reduce-scatter.30
  1591.1 57.4 reduce-scatter.22
  1652.6 69.3 reduce-scatter.34
  1725.9 68.0 reduce-scatter.26
